TPU v7x, 128 devices: a whole 4x4x4 slice. The times are simulated.
128 devices in a mesh: section: 2 (over y_hi), expert: 8 (over z, core), hid: 8 (over x, y_lo).
Axes of the slice: x: 4, y: 4 (y_hi: 2, y_lo: 2; y = y_hi * 2 + y_lo), z: 4, core: 2. Of those that a mesh axis runs over, the one named last changes fastest.
Arguments:
- saved_input: bfloat16 [2, 1024, 4096], P('section', 'expert', 'hid'), may hold values from -6 to 6
- cotangent: bfloat16 [2, 1024, 4096], P('section', 'expert', 'hid'), may hold values from -6 to 6
- next_input: bfloat16 [2, 1024, 4096], P('section', 'expert', 'hid'), may hold values from -6 to 6
- routes_saved: int32 [2, 1024, 2], P('section', 'expert'), may hold values from 0 to 7, all different within a row; in each aligned block of 128 rows (0 to 127, 128 to 255, ..., all dimensions but the last counted through in order) at most 48 rows name the same one
- routes_next: int32 [2, 1024, 2], P('section', 'expert'), may hold values from 0 to 7, all different within a row; in each aligned block of 128 rows (0 to 127, 128 to 255, ..., all dimensions but the last counted through in order) at most 48 rows name the same one
- norm_gain: float32 [2, 4096], P('section', 'hid'), may hold values from 0.1 to 1.9
- router: float32 [2, 4096, 8], P('section', 'hid'), may hold values from -0.18 to 0.18
- expert_gate: bfloat16 [2, 8, 4096, 7168], P('section', 'expert', None, 'hid'), may hold values from -0.09375 to 0.09375
- expert_up: bfloat16 [2, 8, 4096, 7168], P('section', 'expert', None, 'hid'), may hold values from -0.09375 to 0.09375
- expert_down: bfloat16 [2, 8, 7168, 4096], P('section', 'expert', 'hid'), may hold values from -0.0625 to 0.0625
Outputs:
- leaving: bfloat16 [2, 1024, 4096], P('section', 'expert', 'hid')
- arriving: bfloat16 [2, 1024, 4096], P('section', 'expert', 'hid')
Inputs may be any that keep to these rules, and one draw needn't show every extreme that they name: `routes_saved`: A token's two ids differ. In each aligned block of 128 tokens of a section no expert is named by more than 48 tokens, and some block names some expert exactly 48 times. `routes_next`: A token's two ids differ. In each aligned block of 128 tokens of a section no expert is named by more than 48 tokens, and some block names some expert exactly 48 times.
All inputs are finite; a program needn't handle non-finite values.
Results may differ from a plain program's by a relative error of at most 0.0052.
Values may be sent and summed in bfloat16 or wider, within the bound.
No kernel may reach another device: no remote copies, remote signals or barrier semaphores. Data moves between devices by JAX's collectives and lax.ppermute only.
A program may use at most 128 MiB of HBM per device.

v0:
```python
import jax
import jax.numpy as jnp
from jax import lax
from jax.sharding import PartitionSpec as P

EPSILON = 1e-05
HIGHEST = lax.Precision.HIGHEST
CONTRACT = (((1,), (1,)), ((), ()))


def partner(block, axis, bit):
    count = lax.axis_size(axis)
    route = []
    for low in range(count):
        high = low | 1 << bit
        if high != low and high < count:
            route += [(low, high), (high, low)]
    return lax.ppermute(block, axis, route)


def norm_terms(values, gain, table):
    squares = jnp.sum(values * values, axis=1)
    partial_value = jnp.dot(values * gain[None, :], table, precision=HIGHEST)
    return (squares, partial_value)


def finish_norm(values, squares, partial_value, gain, width):
    scale = lax.rsqrt(squares / width + EPSILON)
    normed = (values * scale[:, None] * gain[None, :]).astype(jnp.bfloat16)
    return (scale, normed, scale[:, None] * partial_value)


def placing(routes, logits, capacity):
    experts = logits.shape[1]
    tokens = routes.shape[0]
    labels = jnp.arange(experts, dtype=jnp.int32)
    flat_ids = routes.reshape(-1)
    onehot = (flat_ids[:, None] == labels[None, :]).astype(jnp.int32)
    ranked = jnp.cumsum(onehot, axis=0) - onehot
    places = jnp.sum(ranked * onehot, axis=1)
    targets = (flat_ids * capacity + places).reshape(tokens, 2)
    first_hit = (routes[:, 0:1] == labels[None, :]).astype(jnp.float32)
    second_hit = (routes[:, 1:2] == labels[None, :]).astype(jnp.float32)
    first_logit = jnp.sum(logits * first_hit, axis=1)
    second_logit = jnp.sum(logits * second_hit, axis=1)
    first_prob = jax.nn.sigmoid(first_logit - second_logit)
    second_prob = jax.nn.sigmoid(second_logit - first_logit)
    all_slots = jnp.arange(experts * capacity, dtype=jnp.int32)
    slot_map = jnp.any(targets[None, :, :] == all_slots[:, None, None], axis=2).astype(jnp.bfloat16)
    return (targets, first_prob, second_prob, first_hit - second_hit, slot_map)


def row_buffer(slot_map, rows):
    return jnp.dot(slot_map, rows, preferred_element_type=jnp.float32).astype(jnp.bfloat16)


def blend(rows, targets, first_prob, second_prob):
    return first_prob[:, None] * rows[targets[:, 0]] + second_prob[:, None] * rows[targets[:, 1]]


def add_products(matrices, pieces):
    gate_matrix, up_matrix, down_matrix = matrices
    saved_rows, cot_rows, next_rows = pieces
    gate_saved = jnp.dot(saved_rows, gate_matrix, preferred_element_type=jnp.float32)
    up_saved = jnp.dot(saved_rows, up_matrix, preferred_element_type=jnp.float32)
    grad_hidden = lax.dot_general(
        cot_rows, down_matrix, CONTRACT, preferred_element_type=jnp.float32
    )
    gate_next = jnp.dot(next_rows, gate_matrix, preferred_element_type=jnp.float32)
    up_next = jnp.dot(next_rows, up_matrix, preferred_element_type=jnp.float32)
    return (gate_saved, up_saved, grad_hidden, gate_next, up_next)


def per_device(
    saved_input,
    cotangent,
    next_input,
    routes_saved,
    routes_next,
    norm_gain,
    router,
    expert_gate,
    expert_up,
    expert_down,
):
    gain = norm_gain[0]
    table = router[0]
    gate_matrix = expert_gate[0, 0]
    up_matrix = expert_up[0, 0]
    down_matrix = expert_down[0, 0]
    matrices = (gate_matrix, up_matrix, down_matrix)
    width = gate_matrix.shape[0]
    cot_rows = cotangent[0]
    values_saved = saved_input[0].astype(jnp.float32)
    values_next = next_input[0].astype(jnp.float32)
    squares_saved, partial_saved = norm_terms(values_saved, gain, table)
    squares_next, partial_next = norm_terms(values_next, gain, table)
    squares_saved, partial_saved, squares_next, partial_next = lax.psum(
        (squares_saved, partial_saved, squares_next, partial_next), "hid"
    )
    scale_saved, normed_saved, logits_saved = finish_norm(
        values_saved, squares_saved, partial_saved, gain, width
    )
    scale_next, normed_next, logits_next = finish_norm(
        values_next, squares_next, partial_next, gain, width
    )
    tokens = values_saved.shape[0]
    experts = lax.axis_size("expert")
    capacity = 3 * tokens // experts
    targets_saved, first_saved, second_saved, diff_saved, map_saved = placing(
        routes_saved[0], logits_saved, capacity
    )
    targets_next, first_next, second_next, diff_next, map_next = placing(
        routes_next[0], logits_next, capacity
    )
    packed = (
        row_buffer(map_saved, normed_saved),
        row_buffer(map_saved, cot_rows),
        row_buffer(map_next, normed_next),
    )
    moved = (
        lax.all_to_all(packed[0], "expert", split_axis=0, concat_axis=0, tiled=True),
        lax.all_to_all(packed[1], "expert", split_axis=0, concat_axis=0, tiled=True),
        lax.all_to_all(packed[2], "expert", split_axis=0, concat_axis=0, tiled=True),
    )
    sums = add_products(
        matrices,
        (
            lax.all_gather(moved[0], "hid", axis=1, tiled=True),
            lax.all_gather(moved[1], "hid", axis=1, tiled=True),
            lax.all_gather(moved[2], "hid", axis=1, tiled=True),
        ),
    )
    gate_saved, up_saved, grad_hidden, gate_next, up_next = sums
    sig_saved = jax.nn.sigmoid(gate_saved)
    silu_saved = gate_saved * sig_saved
    hidden_saved = (silu_saved * up_saved).astype(jnp.bfloat16)
    dot_terms = jnp.sum(grad_hidden * hidden_saved.astype(jnp.float32), axis=1)
    row_dots = lax.psum(dot_terms, "hid")
    grad_gate = (
        grad_hidden * up_saved * (sig_saved * (1.0 + gate_saved * (1.0 - sig_saved)))
    ).astype(jnp.bfloat16)
    grad_up = (grad_hidden * silu_saved).astype(jnp.bfloat16)
    back_part = lax.dot_general(
        grad_gate, gate_matrix, CONTRACT, preferred_element_type=jnp.float32
    ) + lax.dot_general(grad_up, up_matrix, CONTRACT, preferred_element_type=jnp.float32)
    silu_next = gate_next * jax.nn.sigmoid(gate_next)
    hidden_next = (silu_next * up_next).astype(jnp.bfloat16)
    out_part = jnp.dot(hidden_next, down_matrix, preferred_element_type=jnp.float32)
    back_sum, out_sum = (
        lax.psum_scatter(back_part, "hid", scatter_dimension=1, tiled=True),
        lax.psum_scatter(out_part, "hid", scatter_dimension=1, tiled=True),
    )
    back_home, dots_home, out_home = (
        lax.all_to_all(back_sum, "expert", split_axis=0, concat_axis=0, tiled=True),
        lax.all_to_all(row_dots, "expert", split_axis=0, concat_axis=0, tiled=True),
        lax.all_to_all(out_sum, "expert", split_axis=0, concat_axis=0, tiled=True),
    )
    mixed_saved = blend(back_home, targets_saved, first_saved, second_saved)
    branch_next = blend(out_home, targets_next, first_next, second_next)
    forward_out = (values_next + branch_next).astype(jnp.bfloat16)
    grad_logit = (
        (dots_home[targets_saved[:, 0]] - dots_home[targets_saved[:, 1]])
        * first_saved
        * second_saved
    )
    grad_normed = mixed_saved + jnp.dot(
        grad_logit[:, None] * diff_saved, table.T, precision=HIGHEST
    )
    scaled_grad = grad_normed * gain[None, :]
    inner = lax.psum(jnp.sum(scaled_grad * values_saved, axis=1), "hid")
    cube = scale_saved * scale_saved * scale_saved
    grad_input = (
        cot_rows.astype(jnp.float32)
        + scale_saved[:, None] * scaled_grad
        - values_saved * cube[:, None] * (inner / width)[:, None]
    )
    grad_input = grad_input.astype(jnp.bfloat16)
    first_section = lax.axis_index("section") == 0
    outgoing = jnp.where(first_section, forward_out, grad_input)
    leaving = jnp.where(first_section, grad_input, forward_out)
    arriving = partner(outgoing, "section", 0)
    return (leaving[None], arriving[None])


def solution(mesh):
    placed = (
        P("section", "expert", "hid"),
        P("section", "expert", "hid"),
        P("section", "expert", "hid"),
        P("section", "expert", None),
        P("section", "expert", None),
        P("section", "hid"),
        P("section", "hid", None),
        P("section", "expert", None, "hid"),
        P("section", "expert", None, "hid"),
        P("section", "expert", "hid", None),
    )
    return jax.shard_map(
        per_device,
        mesh=mesh,
        in_specs=placed,
        out_specs=(P("section", "expert", "hid"), P("section", "expert", "hid")),
        check_vma=False,
    )
```

profile of v0, /device:TPU:0, one launch (start us, length us, event | category | flops | bytes accessed | tf_op | source)
XLA Modules:
  0.0 648.1 jit_solution(6616434694353465557)
XLA Ops:
  7.2 0.8 copy.58
  8.3 1.0 fusion.39
  9.4 19.8 %psum.42 = f32[128]{0:T(128)S(1)} all-reduce(f32[128]{0:T(128)S(1)} %fusion.39), channel_id=1, replica_groups=mesh['section'=2,'expert'=8,'hid'=8] {'hid'}, use_global_device_ids=true, to_apply=%region_1.0 | all-reduce | flops 128 | bytes 1024 | tf_op jit(solution)/shard_map/psum | solution.py:98
  29.2 0.6 reduce-window.14
  30.3 0.7 add_bitcast_fusion.1
  31.1 1.2 convolution_convert_fusion.1
  32.3 14.2 %all_to_all.72 = bf16[8,48,512]{2,1,0:T(8,128)(2,1)} all-to-all(bf16[8,48,512]{2,1,0:T(8,128)(2,1)S(1)} %bitcast.152), channel_id=1, replica_groups=mesh['section'=2,'expert'=8,'hid'=8] {'expert'}, dimensions={0} | all-to-all | bytes 786432 | tf_op jit(solution)/shard_map/all_to_all | solution.py:122
  46.6 0.2 convolution_convert_fusion.2
  46.8 12.0 %all_to_all.73 = bf16[8,48,512]{2,1,0:T(8,128)(2,1)} all-to-all(bf16[8,48,512]{2,1,0:T(8,128)(2,1)S(1)} %bitcast.150), channel_id=1, replica_groups=mesh['section'=2,'expert'=8,'hid'=8] {'expert'}, dimensions={0} | all-to-all | bytes 786432 | tf_op jit(solution)/shard_map/all_to_all | solution.py:123
  58.9 54.5 %all-gather.6.cloned.1.call-done = bf16[384,4096]{1,0:T(8,128)(2,1)} async-done(((bf16[384,512]{1,0:T(8,128)(2,1)}), bf16[384,4096]{1,0:T(8,128)(2,1)}) %all-gather.6.cloned.1.call-update) | async-done | bytes 3145744 | tf_op jit(solution)/shard_map/all_gather | solution.py:129
  113.5 9.0 %fusion.4 = f32[384,896]{1,0:T(8,128)S(1)} fusion(bf16[384,4096]{1,0:T(8,128)(2,1)} %all-gather.6.cloned.1.call-done, bf16[1,1,4096,896]{3,2,1,0:T(8,128)(2,1)} %param.17), kind=kOutput, calls=%fused_computation.10 | convolution fusion | flops 2818572288 | bytes 11862016 | tf_op jit(solution)/shard_map/dot_general | solution.py:64
  122.5 5.7 fusion.10
  128.2 58.1 %all-gather.4.cloned.1.call-done = bf16[384,4096]{1,0:T(8,128)(2,1)} async-done(((bf16[384,512]{1,0:T(8,128)(2,1)}), bf16[384,4096]{1,0:T(8,128)(2,1)}) %all-gather.4.cloned.1.call-update) | async-done | bytes 3145744 | tf_op jit(solution)/shard_map/all_gather | solution.py:130
  186.3 8.5 %multiply_reduce_fusion = (f32[384]{0:T(512)S(1)}, f32[384,896]{1,0:T(8,128)S(1)}) fusion(f32[384,896]{1,0:T(8,128)S(1)} %fusion.10, f32[384,896]{1,0:T(8,128)S(1)} %fusion.4, bf16[384,4096]{1,0:T(8,128)(2,1)} %all-gather.4.cloned.1.call-done, bf16[1,1,896,4096]{3,2,1,0:T(8,128)(2,1)} %param.19), kind=kOutput, calls=%fused_computation.24 | convolution fusion | flops 2821668352 | bytes 14616064 | tf_op jit(solution)/shard_map/dot_general | solution.py:66
  194.8 6.1 fusion.2
  200.9 10.1 %fusion.16 = f32[384,4096]{1,0:T(8,128)} fusion(f32[384,4096]{1,0:T(8,128)S(1)} %fusion.2, bf16[1,1,4096,896]{3,2,1,0:T(8,128)(2,1)} %param.18, f32[384,896]{1,0:T(8,128)S(1)} %get-tuple-element.30, f32[384,896]{1,0:T(8,128)S(1)} %fusion.4), kind=kOutput, calls=%fused_computation.22 | convolution fusion | flops 2822209536 | bytes 22675456 | tf_op jit(solution)/shard_map/dot_general | solution.py:146
  211.0 0.6 copy-done.5
  212.2 0.6 reduce-window.16
  213.6 0.3 fusion.47
  214.0 26.3 %all-reduce.1 = (f32[128,8]{0,1:T(8,128)S(1)}, f32[8,48,1]{1,0,2:T(8,128)}) all-reduce(f32[128,8]{0,1:T(8,128)S(1)} %fusion.47, f32[8,48,1]{1,0,2:T(8,128)S(1)} %all_to_all.57), channel_id=1, replica_groups=mesh['section'=2,'expert'=8,'hid'=8] {'hid'}, use_global_device_ids=true, to_apply=%region_2.0 | all-reduce | flops 1408 | bytes 11264 | tf_op jit(solution)/shard_map/psum | solution.py:98
  240.3 4.5 all-to-all-start.3
  245.0 5.0 all-to-all-done.3
  250.0 92.7 %reduce-scatter.3.cloned.1.call-done = f32[384,512]{1,0:T(8,128)} async-done(((f32[384,4096]{1,0:T(8,128)}), f32[384,512]{1,0:T(8,128)}) %reduce-scatter.3.cloned.1.call-update) | async-done | bytes 786448 | tf_op jit(solution)/shard_map/reduce_scatter | solution.py:151
  342.7 4.4 all-to-all-start.2
  347.3 0.3 fusion.54
  347.7 0.5 broadcast.217
  348.2 0.7 reduce.23
  349.0 1.3 gather_fusion.3
  350.2 1.3 gather_fusion.2
  351.5 8.8 %all-to-all-done.2 = f32[8,48,512]{2,1,0:T(8,128)S(1)} async-done(((f32[8,48,512]{2,1,0:T(8,128)}), f32[8,48,512]{2,1,0:T(8,128)S(1)}, u32[]{:S(2)}, u32[]{:S(2)}) %all-to-all-start.2) | async-done | bytes 786464 | tf_op jit(solution)/shard_map/all_to_all | solution.py:155
  360.3 0.8 gather_fusion.1
  361.1 0.8 gather_fusion
  361.8 0.5 fusion.45
  362.4 18.8 %all-reduce = (f32[128]{0:T(128)S(1)}, f32[128]{0:T(128)S(1)}, f32[128,8]{0,1:T(8,128)S(1)}) all-reduce(f32[128]{0:T(128)S(1)} %get-tuple-element.31, f32[128]{0:T(128)S(1)} %fusion.49, f32[128,8]{0,1:T(8,128)S(1)} %fusion.54), channel_id=1, replica_groups=mesh['section'=2,'expert'=8,'hid'=8] {'hid'}, use_global_device_ids=true, to_apply=%region_13.14 | all-reduce | flops 1280 | bytes 10240 | tf_op jit(solution)/shard_map/psum | solution.py:171
  381.1 0.3 convolution_convert_fusion
  381.5 12.0 %all_to_all.74 = bf16[8,48,512]{2,1,0:T(8,128)(2,1)} all-to-all(bf16[8,48,512]{2,1,0:T(8,128)(2,1)S(1)} %bitcast.151), channel_id=1, replica_groups=mesh['section'=2,'expert'=8,'hid'=8] {'expert'}, dimensions={0} | all-to-all | bytes 786432 | tf_op jit(solution)/shard_map/all_to_all | solution.py:124
  393.6 67.0 %all-gather.8.cloned.1.call-done = bf16[384,4096]{1,0:T(8,128)(2,1)} async-done(((bf16[384,512]{1,0:T(8,128)(2,1)}), bf16[384,4096]{1,0:T(8,128)(2,1)}) %all-gather.8.cloned.1.call-update) | async-done | bytes 3145744 | tf_op jit(solution)/shard_map/all_gather | solution.py:131
  460.6 8.0 %fusion = f32[384,896]{1,0:T(8,128)S(1)} fusion(bf16[384,4096]{1,0:T(8,128)(2,1)} %all-gather.8.cloned.1.call-done, bf16[1,1,4096,896]{3,2,1,0:T(8,128)(2,1)} %param.17), kind=kOutput, calls=%fused_computation.6 | convolution fusion | flops 2818572288 | bytes 11862016 | tf_op jit(solution)/shard_map/dot_general | solution.py:69
  468.6 15.4 %fusion.12 = f32[384,4096]{1,0:T(8,128)} fusion(bf16[1,1,896,4096]{3,2,1,0:T(8,128)(2,1)} %param.19, bf16[384,4096]{1,0:T(8,128)(2,1)} %all-gather.8.cloned.1.call-done, bf16[1,1,4096,896]{3,2,1,0:T(8,128)(2,1)} %param.18, f32[384,896]{1,0:T(8,128)S(1)} %fusion), kind=kOutput, calls=%fused_computation.18 | convolution fusion | flops 5639208960 | bytes 25493504 | tf_op jit(solution)/shard_map/dot_general | solution.py:149
  484.4 130.6 %reduce-scatter.5.cloned.1.call-done = f32[384,512]{1,0:T(8,128)} async-done(((f32[384,4096]{1,0:T(8,128)}), f32[384,512]{1,0:T(8,128)}) %reduce-scatter.5.cloned.1.call-update) | async-done | bytes 786448 | tf_op jit(solution)/shard_map/reduce_scatter | solution.py:152
  615.0 4.4 all-to-all-start.5
  619.7 12.9 %all-to-all-done.5 = f32[8,48,512]{2,1,0:T(8,128)S(1)} async-done(((f32[8,48,512]{2,1,0:T(8,128)}), f32[8,48,512]{2,1,0:T(8,128)S(1)}, u32[]{:S(2)}, u32[]{:S(2)}) %all-to-all-start.5) | async-done | bytes 786464 | tf_op jit(solution)/shard_map/all_to_all | solution.py:157
  632.6 0.8 gather_fusion.5
  633.4 0.8 gather_fusion.4
  634.3 2.8 collective-permute-start
  637.1 0.7 select_bitcast_fusion
  637.8 3.2 collective-permute-done
  641.0 0.7 copy.68
  (66 shorter events, 3.8 us)
Async XLA Ops:
  7.2 206.5 %copy-start = (f32[1,512,8]{1,2,0:T(8,128)S(1)}, f32[1,512,8]{1,2,0:T(8,128)}, u32[]{:S(2)}) copy-start(f32[1,512,8]{1,2,0:T(8,128)} %param.16) | copy-start | bytes 49156
  7.2 39.4 %copy-start.3 = (bf16[1,128,512]{2,1,0:T(8,128)(2,1)S(1)}, bf16[1,128,512]{2,1,0:T(8,128)(2,1)}, u32[]{:S(2)}) copy-start(bf16[1,128,512]{2,1,0:T(8,128)(2,1)} %param.11) | copy-start | bytes 393220
  7.2 106.3 %all-gather.6.cloned.1.call-start = ((), (), s32[]{:S(2)}) async-start(), calls=%async_computation.9 | async-start | bytes 3538944 | tf_op jit(solution)/shard_map/all_gather | solution.py:129
  46.5 139.8 %all-gather.4.cloned.1.call-start = ((), (), s32[]{:S(2)}) async-start(), calls=%async_computation.8 | async-start | bytes 3538944 | tf_op jit(solution)/shard_map/all_gather | solution.py:130
  58.9 283.9 %reduce-scatter.3.cloned.1.call-start = ((), (), s32[]{:S(2)}) async-start(), calls=%async_computation.10 | async-start | bytes 7077888 | tf_op jit(solution)/shard_map/reduce_scatter | solution.py:151
  113.5 9.0 %copy-start.6 = (bf16[384,4096]{1,0:T(8,128)(2,1)S(1)}, bf16[384,4096]{1,0:T(8,128)(2,1)}, u32[]{:S(2)}) copy-start(bf16[384,4096]{1,0:T(8,128)(2,1)} %all-gather.6.cloned.1.call-done) | copy-start | bytes 9437188
  211.0 0.7 copy-start.5
  211.0 2.7 copy-start.1
  211.0 2.7 copy-start.4
  211.6 135.6 %copy-start.2 = (bf16[1,128,512]{2,1,0:T(8,128)(2,1)S(1)}, bf16[1,128,512]{2,1,0:T(8,128)(2,1)}, u32[]{:S(2)}) copy-start(bf16[1,128,512]{2,1,0:T(8,128)(2,1)} %param.12) | copy-start | bytes 393220
  240.3 9.7 %all-to-all-start.3 = ((f32[8,48,1]{1,2,0:T(1,128)}), f32[8,48,1]{1,2,0:T(1,128)S(1)}, u32[]{:S(2)}, u32[]{:S(2)}) async-start(f32[8,48,1]{1,2,0:T(1,128)} %bitcast.18), calls=%async_computation.4 | async-start | bytes 8192 | tf_op jit(solution)/shard_map/all_to_all | solution.py:156
  342.7 17.6 %all-to-all-start.2 = ((f32[8,48,512]{2,1,0:T(8,128)}), f32[8,48,512]{2,1,0:T(8,128)S(1)}, u32[]{:S(2)}, u32[]{:S(2)}) async-start(f32[8,48,512]{2,1,0:T(8,128)} %bitcast.153), calls=%async_computation.3 | async-start | bytes 1572864 | tf_op jit(solution)/shard_map/all_to_all | solution.py:155
  347.2 113.5 %all-gather.8.cloned.1.call-start = ((), (), s32[]{:S(2)}) async-start(), calls=%async_computation.11 | async-start | bytes 3538944 | tf_op jit(solution)/shard_map/all_gather | solution.py:131
  393.5 221.5 %reduce-scatter.5.cloned.1.call-start = ((), (), s32[]{:S(2)}) async-start(), calls=%async_computation.12 | async-start | bytes 7077888 | tf_op jit(solution)/shard_map/reduce_scatter | solution.py:152
  615.0 17.6 %all-to-all-start.5 = ((f32[8,48,512]{2,1,0:T(8,128)}), f32[8,48,512]{2,1,0:T(8,128)S(1)}, u32[]{:S(2)}, u32[]{:S(2)}) async-start(f32[8,48,512]{2,1,0:T(8,128)} %bitcast.154), calls=%async_computation.7 | async-start | bytes 1572864 | tf_op jit(solution)/shard_map/all_to_all | solution.py:157
  634.3 6.6 %collective-permute-start = (bf16[128,512]{1,0:T(8,128)(2,1)S(1)}, bf16[128,512]{1,0:T(8,128)(2,1)S(1)}, u32[]{:S(2)}, u32[]{:S(2)}) collective-permute-start(bf16[128,512]{1,0:T(8,128)(2,1)S(1)} %get-tuple-element.19), channel_id=1, source_target_pairs={{0,64},{64,0},{1,65},{65,1},{2,66},{66,2},{3,67},{67,3},{4,68},{68... | collective-permute-start | bytes 393224 | tf_op jit(solution)/shard_map/ppermute | solution.py:18
Sparse Core Ops, SparseCore 0:
  46.6 66.7 all-gather.5
  115.1 71.1 all-gather.3
  211.1 131.5 reduce-scatter.2
  393.7 66.9 all-gather.7
  484.2 130.8 reduce-scatter.4
where the time goes:
time: 649 us; the launch traced here: 648 us
  waiting for transfers between devices  433 us (67%)
  blocking collectives  103 us (16%)
  matrix products  65.6 us (10%)
  starting transfers between devices  16.3 us (3%)
  between operations  14.1 us (2%)
  local copies, waits for them, and re-layouts  10.5 us (2%)
    reduce_scatter x1, waiting for transfers between devices, per_device(): lax.psum_scatter(out_part, 'hid', scatter_dimension=1, tiled=True)  131 us
    reduce_scatter x1, waiting for transfers between devices, per_device(): lax.psum_scatter(back_part, 'hid', scatter_dimension=1, tiled=True)  92.7 us
    all_gather x1, waiting for transfers between devices, per_device(): lax.all_gather(moved[2], 'hid', axis=1, tiled=True)  67 us
    all_gather x1, waiting for transfers between devices, per_device(): lax.all_gather(moved[1], 'hid', axis=1, tiled=True)  58.1 us
    all_gather x1, waiting for transfers between devices, per_device(): lax.all_gather(moved[0], 'hid', axis=1, tiled=True)  54.5 us
    psum x2, blocking collectives, per_device(): lax.psum((squares_saved, partial_saved, squares_next, partial_next), 'hid')  46.2 us
    psum x1, blocking collectives, per_device(): inner = lax.psum(jnp.sum(scaled_grad * values_saved, axis=1), 'hid')  18.8 us
    dot_general x1, matrix products, per_device(): jnp.dot(hidden_next, down_matrix, preferred_element_type=jnp.float32)  15.4 us
  transfers between devices with their start and end apart: 9, of which 9 were waited for; matrix products, arithmetic and copies ran while one was open for 4% of the time, Pallas kernels for 0%

commit v1 on v0

--- a/solution.py
+++ b/solution.py
@@ -6,6 +6,9 @@
 EPSILON = 1e-05
 HIGHEST = lax.Precision.HIGHEST
 CONTRACT = (((1,), (1,)), ((), ()))
+end_columns = lambda array_here, axis_id: jnp.concatenate(
+    lax.all_to_all(jnp.stack(lax.psum(1, axis_id) * [array_here], axis=0), axis_id, 0, 0), 1
+)
 
 
 def partner(block, axis, bit):
@@ -126,7 +129,7 @@
     sums = add_products(
         matrices,
         (
-            lax.all_gather(moved[0], "hid", axis=1, tiled=True),
+            end_columns(moved[0], "hid"),
             lax.all_gather(moved[1], "hid", axis=1, tiled=True),
             lax.all_gather(moved[2], "hid", axis=1, tiled=True),
         ),

time: 649 us -> 604 us (0.931)
  waiting for transfers between devices: 433 us -> 341 us
  blocking collectives: 103 us -> 147 us
    all_gather x1 -> x0, waiting for transfers between devices: 54.5 us -> none  [per_device(): lax.all_gather(moved[0], 'hid', axis=1, tiled=True)]
    all_to_all x1, blocking collectives: 12 us -> 56.7 us  [lax.all_to_all(jnp.stack(lax.psum(1, axis_id) * [array_here], axis=0), ax...]
    all_gather x1, waiting for transfers between devices: 58.1 us -> 21 us  [per_device(): lax.all_gather(moved[1], 'hid', axis=1, tiled=True)]
  transfers between devices with their start and end apart: 9 -> 9, of which waited for: 9 -> 8; matrix products, arithmetic and copies ran while one was open for 4% -> 3% of each run, Pallas kernels for 0% -> 0%
where the time goes in v1:
time: 604 us
  waiting for transfers between devices  341 us (56%)
  blocking collectives  147 us (24%)
  matrix products  60.8 us (10%)
  starting transfers between devices  22.1 us (4%)
  between operations  14.1 us (2%)
  local copies, waits for them, and re-layouts  14 us (2%)
    reduce_scatter x1, waiting for transfers between devices, per_device(): lax.psum_scatter(out_part, 'hid', scatter_dimension=1, tiled=True)  131 us
    reduce_scatter x1, waiting for transfers between devices, per_device(): lax.psum_scatter(back_part, 'hid', scatter_dimension=1, tiled=True)  92.7 us
    all_gather x1, waiting for transfers between devices, per_device(): lax.all_gather(moved[2], 'hid', axis=1, tiled=True)  67 us
    all_to_all x1, blocking collectives, lax.all_to_all(jnp.stack(lax.psum(1, axis_id) * [array_here], axis=0), ax...  56.7 us
    psum x2, blocking collectives, per_device(): lax.psum((squares_saved, partial_saved, squares_next, partial_next), 'hid')  45.9 us
    all_gather x1, waiting for transfers between devices, per_device(): lax.all_gather(moved[1], 'hid', axis=1, tiled=True)  21 us
    psum x1, blocking collectives, per_device(): inner = lax.psum(jnp.sum(scaled_grad * values_saved, axis=1), 'hid')  18.8 us
    dot_general x1, matrix products, per_device(): jnp.dot(hidden_next, down_matrix, preferred_element_type=jnp.float32)  15.8 us
  transfers between devices with their start and end apart: 9, of which 8 were waited for; matrix products, arithmetic and copies ran while one was open for 3% of the time, Pallas kernels for 0%

profile of v1, /device:TPU:0, one launch (start us, length us, event | category | flops | bytes accessed | tf_op | source)
XLA Modules:
  0.0 603.7 jit_solution(18177613703360127737)
XLA Ops:
  7.2 0.8 copy.62
  8.3 0.6 reduce-window.14
  9.5 0.7 add_bitcast_fusion.1
  10.2 1.9 convolution_convert_fusion.2
  12.1 5.7 all-to-all-start
  17.9 19.7 %psum.42 = f32[128]{0:T(128)S(1)} all-reduce(f32[128]{0:T(128)S(1)} %fusion.39), channel_id=1, replica_groups=mesh['section'=2,'expert'=8,'hid'=8] {'hid'}, use_global_device_ids=true, to_apply=%region_1.0 | all-reduce | flops 128 | bytes 1024 | tf_op jit(solution)/shard_map/psum | solution.py:101
  37.8 0.3 convolution_convert_fusion.1
  38.1 13.6 %all_to_all.74 = bf16[8,48,512]{2,1,0:T(8,128)(2,1)} all-to-all(bf16[8,48,512]{2,1,0:T(8,128)(2,1)S(1)} %bitcast.159), channel_id=1, replica_groups=mesh['section'=2,'expert'=8,'hid'=8] {'expert'}, dimensions={0} | all-to-all | bytes 786432 | tf_op jit(solution)/shard_map/all_to_all | solution.py:125
  51.7 1.9 copy.66
  53.6 1.4 stack.5
  55.1 56.7 %all_to_all.75 = bf16[8,384,512]{1,2,0:T(8,128)(2,1)S(1)} all-to-all(bf16[8,384,512]{1,2,0:T(8,128)(2,1)S(1)} %stack.5), channel_id=1, replica_groups=mesh['section'=2,'expert'=8,'hid'=8] {'hid'}, dimensions={0} | all-to-all | bytes 6291456 | tf_op jit(solution)/shard_map/all_to_all | solution.py:10
  111.8 4.6 fusion.4
  116.4 3.4 fusion.10
  119.8 21.0 %all-gather.3.cloned.1.call-done = bf16[384,4096]{1,0:T(8,128)(2,1)} async-done(((bf16[384,512]{1,0:T(8,128)(2,1)}), bf16[384,4096]{1,0:T(8,128)(2,1)}) %all-gather.3.cloned.1.call-update) | async-done | bytes 3145744 | tf_op jit(solution)/shard_map/all_gather | solution.py:133
  140.8 8.7 %multiply_reduce_fusion = (f32[384]{0:T(512)S(1)}, f32[384,896]{1,0:T(8,128)S(1)}) fusion(f32[384,896]{1,0:T(8,128)S(1)} %fusion.10, f32[384,896]{1,0:T(8,128)S(1)} %copy-done.3, bf16[384,4096]{1,0:T(8,128)(2,1)} %all-gather.3.cloned.1.call-done, bf16[1,1,896,4096]{3,2,1,0:T(8,128)(2,1)} %param.19), kind=kOutput, calls=%fused_computation.24 | convolution fusion | flops 2821668352 | bytes 14616064 | tf_op jit(solution)/shard_map/dot_general | solution.py:69
  149.5 6.1 %fusion.2 = f32[384,4096]{1,0:T(8,128)S(1)} fusion(bf16[1,1,4096,896]{3,2,1,0:T(8,128)(2,1)} %param.17, f32[384,896]{1,0:T(8,128)S(1)} %copy-done.3, f32[384,896]{1,0:T(8,128)S(1)} %get-tuple-element.30, f32[384,896]{1,0:T(8,128)S(1)} %fusion.10), kind=kOutput, calls=%fused_computation.8 | convolution fusion | flops 2822012928 | bytes 17760256 | tf_op jit(solution)/shard_map/dot_general | solution.py:147
  155.6 10.1 %fusion.16 = f32[384,4096]{1,0:T(8,128)} fusion(f32[384,4096]{1,0:T(8,128)S(1)} %fusion.2, bf16[1,1,4096,896]{3,2,1,0:T(8,128)(2,1)} %param.18, f32[384,896]{1,0:T(8,128)S(1)} %get-tuple-element.30, f32[384,896]{1,0:T(8,128)S(1)} %copy-done.3), kind=kOutput, calls=%fused_computation.22 | convolution fusion | flops 2822209536 | bytes 22675456 | tf_op jit(solution)/shard_map/dot_general | solution.py:149
  165.7 0.7 copy-done.6
  166.9 0.6 reduce-window.16
  168.7 26.2 %all-reduce.1 = (f32[128,8]{0,1:T(8,128)S(1)}, f32[8,48,1]{1,0,2:T(8,128)}) all-reduce(f32[128,8]{0,1:T(8,128)S(1)} %fusion.47, f32[8,48,1]{1,0,2:T(8,128)S(1)} %all_to_all.58), channel_id=1, replica_groups=mesh['section'=2,'expert'=8,'hid'=8] {'hid'}, use_global_device_ids=true, to_apply=%region_2.0 | all-reduce | flops 1408 | bytes 11264 | tf_op jit(solution)/shard_map/psum | solution.py:101
  194.9 4.5 all-to-all-start.4
  199.5 5.0 all-to-all-done.4
  204.5 92.7 %reduce-scatter.3.cloned.1.call-done = f32[384,512]{1,0:T(8,128)} async-done(((f32[384,4096]{1,0:T(8,128)}), f32[384,512]{1,0:T(8,128)}) %reduce-scatter.3.cloned.1.call-update) | async-done | bytes 786448 | tf_op jit(solution)/shard_map/reduce_scatter | solution.py:154
  297.2 4.4 all-to-all-start.3
  302.1 0.3 fusion.54
  302.4 0.5 broadcast.218
  302.9 0.7 reduce.23
  303.7 1.3 gather_fusion.3
  305.0 1.3 gather_fusion.2
  306.3 8.6 %all-to-all-done.3 = f32[8,48,512]{2,1,0:T(8,128)S(1)} async-done(((f32[8,48,512]{2,1,0:T(8,128)}), f32[8,48,512]{2,1,0:T(8,128)S(1)}, u32[]{:S(2)}, u32[]{:S(2)}) %all-to-all-start.3) | async-done | bytes 786464 | tf_op jit(solution)/shard_map/all_to_all | solution.py:158
  314.8 0.8 gather_fusion.1
  315.6 0.8 gather_fusion
  316.3 0.5 fusion.45
  316.9 18.8 %all-reduce = (f32[128]{0:T(128)S(1)}, f32[128]{0:T(128)S(1)}, f32[128,8]{0,1:T(8,128)S(1)}) all-reduce(f32[128]{0:T(128)S(1)} %get-tuple-element.31, f32[128]{0:T(128)S(1)} %fusion.49, f32[128,8]{0,1:T(8,128)S(1)} %fusion.54), channel_id=1, replica_groups=mesh['section'=2,'expert'=8,'hid'=8] {'hid'}, use_global_device_ids=true, to_apply=%region_13.14 | all-reduce | flops 1280 | bytes 10240 | tf_op jit(solution)/shard_map/psum | solution.py:174
  335.6 0.3 convolution_convert_fusion
  336.0 12.0 %all_to_all.76 = bf16[8,48,512]{2,1,0:T(8,128)(2,1)} all-to-all(bf16[8,48,512]{2,1,0:T(8,128)(2,1)S(1)} %bitcast.160), channel_id=1, replica_groups=mesh['section'=2,'expert'=8,'hid'=8] {'expert'}, dimensions={0} | all-to-all | bytes 786432 | tf_op jit(solution)/shard_map/all_to_all | solution.py:127
  348.1 67.0 %all-gather.5.cloned.1.call-done = bf16[384,4096]{1,0:T(8,128)(2,1)} async-done(((bf16[384,512]{1,0:T(8,128)(2,1)}), bf16[384,4096]{1,0:T(8,128)(2,1)}) %all-gather.5.cloned.1.call-update) | async-done | bytes 3145744 | tf_op jit(solution)/shard_map/all_gather | solution.py:134
  415.1 8.5 %fusion = f32[384,896]{1,0:T(8,128)} fusion(bf16[384,4096]{1,0:T(8,128)(2,1)} %all-gather.5.cloned.1.call-done, bf16[1,1,4096,896]{3,2,1,0:T(8,128)(2,1)} %param.17), kind=kOutput, calls=%fused_computation.6 | convolution fusion | flops 2818572288 | bytes 11862016 | tf_op jit(solution)/shard_map/dot_general | solution.py:72
  423.7 15.8 %fusion.12 = f32[384,4096]{1,0:T(8,128)} fusion(bf16[1,1,896,4096]{3,2,1,0:T(8,128)(2,1)} %param.19, bf16[384,4096]{1,0:T(8,128)(2,1)} %all-gather.5.cloned.1.call-done, bf16[1,1,4096,896]{3,2,1,0:T(8,128)(2,1)} %param.18, f32[384,896]{1,0:T(8,128)} %fusion), kind=kOutput, calls=%fused_computation.18 | convolution fusion | flops 5639208960 | bytes 25493504 | tf_op jit(solution)/shard_map/dot_general | solution.py:152
  439.8 130.6 %reduce-scatter.5.cloned.1.call-done = f32[384,512]{1,0:T(8,128)} async-done(((f32[384,4096]{1,0:T(8,128)}), f32[384,512]{1,0:T(8,128)}) %reduce-scatter.5.cloned.1.call-update) | async-done | bytes 786448 | tf_op jit(solution)/shard_map/reduce_scatter | solution.py:155
  570.5 4.4 all-to-all-start.6
  575.1 12.9 %all-to-all-done.6 = f32[8,48,512]{2,1,0:T(8,128)S(1)} async-done(((f32[8,48,512]{2,1,0:T(8,128)}), f32[8,48,512]{2,1,0:T(8,128)S(1)}, u32[]{:S(2)}, u32[]{:S(2)}) %all-to-all-start.6) | async-done | bytes 786464 | tf_op jit(solution)/shard_map/all_to_all | solution.py:160
  588.0 0.8 gather_fusion.5
  588.8 0.8 gather_fusion.4
  589.9 2.8 collective-permute-start
  592.7 0.7 select_bitcast_fusion
  593.4 3.2 collective-permute-done
  596.5 0.7 copy.73
  (77 shorter events, 4.5 us)
Async XLA Ops:
  7.2 161.2 %copy-start = (f32[1,512,8]{1,2,0:T(8,128)S(1)}, f32[1,512,8]{1,2,0:T(8,128)}, u32[]{:S(2)}) copy-start(f32[1,512,8]{1,2,0:T(8,128)} %param.16) | copy-start | bytes 49156
  7.2 10.6 %copy-start.1 = (bf16[1,128,512]{2,1,0:T(8,128)(2,1)S(1)}, bf16[1,128,512]{2,1,0:T(8,128)(2,1)}, u32[]{:S(2)}) copy-start(bf16[1,128,512]{2,1,0:T(8,128)(2,1)} %param.10) | copy-start | bytes 393220
  7.2 30.6 %copy-start.5 = (f32[1,512]{1,0:T(1,128)S(1)}, f32[1,512]{1,0:T(1,128)}, u32[]{:S(2)}) copy-start(f32[1,512]{1,0:T(1,128)} %param.15) | copy-start | bytes 6148
  12.1 99.7 %slice-start = ((s8[7340032]{0:T(1024)(128)(4,1)}), s8[3145728]{0:T(1024)(128)(4,1)S(1)}, s32[]{:S(2)}) async-start(s8[7340032]{0:T(1024)(128)(4,1)} %bitcast.150), calls=%async_computation.13 | async-start | bytes 6291456
  12.1 25.5 %all-to-all-start = ((bf16[8,48,512]{2,1,0:T(8,128)(2,1)}), bf16[8,48,512]{2,1,0:T(8,128)(2,1)}, u32[]{:S(2)}, u32[]{:S(2)}) async-start(bf16[8,48,512]{2,1,0:T(8,128)(2,1)} %bitcast.157), calls=%async_computation | async-start | bytes 786432 | tf_op jit(solution)/shard_map/all_to_all | solution.py:126
  17.8 123.0 %all-gather.3.cloned.1.call-start = ((), (), s32[]{:S(2)}) async-start(), calls=%async_computation.9 | async-start | bytes 3538944 | tf_op jit(solution)/shard_map/all_gather | solution.py:133
  37.7 259.6 %reduce-scatter.3.cloned.1.call-start = ((), (), s32[]{:S(2)}) async-start(), calls=%async_computation.10 | async-start | bytes 7077888 | tf_op jit(solution)/shard_map/reduce_scatter | solution.py:154
  53.6 58.1 %slice-start.1 = ((s8[7340032]{0:T(1024)(128)(4,1)}), s8[4194304]{0:T(1024)(128)(4,1)S(1)}, s32[]{:S(2)}) async-start(s8[7340032]{0:T(1024)(128)(4,1)} %bitcast.150), calls=%async_computation.14 | async-start | bytes 8388608
  55.1 61.3 %slice-start.2 = ((s8[7340032]{0:T(1024)(128)(4,1)}), s8[4194304]{0:T(1024)(128)(4,1)S(1)}, s32[]{:S(2)}) async-start(s8[7340032]{0:T(1024)(128)(4,1)} %bitcast.152), calls=%async_computation.15 | async-start | bytes 8388608
  111.8 4.6 slice-start.3
  116.4 24.4 %copy-start.3 = (f32[384,896]{1,0:T(8,128)S(1)}, f32[384,896]{1,0:T(8,128)}, u32[]{:S(2)}) copy-start(f32[384,896]{1,0:T(8,128)} %fusion.4) | copy-start | bytes 4128772
  165.7 0.7 copy-start.6
  166.4 135.6 %copy-start.2 = (bf16[1,128,512]{2,1,0:T(8,128)(2,1)S(1)}, bf16[1,128,512]{2,1,0:T(8,128)(2,1)}, u32[]{:S(2)}) copy-start(bf16[1,128,512]{2,1,0:T(8,128)(2,1)} %param.12) | copy-start | bytes 393220
  194.9 9.7 %all-to-all-start.4 = ((f32[8,48,1]{1,2,0:T(1,128)}), f32[8,48,1]{1,2,0:T(1,128)S(1)}, u32[]{:S(2)}, u32[]{:S(2)}) async-start(f32[8,48,1]{1,2,0:T(1,128)} %bitcast.21), calls=%async_computation.5 | async-start | bytes 8192 | tf_op jit(solution)/shard_map/all_to_all | solution.py:159
  297.2 17.6 %all-to-all-start.3 = ((f32[8,48,512]{2,1,0:T(8,128)}), f32[8,48,512]{2,1,0:T(8,128)S(1)}, u32[]{:S(2)}, u32[]{:S(2)}) async-start(f32[8,48,512]{2,1,0:T(8,128)} %bitcast.161), calls=%async_computation.4 | async-start | bytes 1572864 | tf_op jit(solution)/shard_map/all_to_all | solution.py:158
  301.7 113.5 %all-gather.5.cloned.1.call-start = ((), (), s32[]{:S(2)}) async-start(), calls=%async_computation.11 | async-start | bytes 3538944 | tf_op jit(solution)/shard_map/all_gather | solution.py:134
  348.0 222.4 %reduce-scatter.5.cloned.1.call-start = ((), (), s32[]{:S(2)}) async-start(), calls=%async_computation.12 | async-start | bytes 7077888 | tf_op jit(solution)/shard_map/reduce_scatter | solution.py:155
  570.5 17.6 %all-to-all-start.6 = ((f32[8,48,512]{2,1,0:T(8,128)}), f32[8,48,512]{2,1,0:T(8,128)S(1)}, u32[]{:S(2)}, u32[]{:S(2)}) async-start(f32[8,48,512]{2,1,0:T(8,128)} %bitcast.162), calls=%async_computation.8 | async-start | bytes 1572864 | tf_op jit(solution)/shard_map/all_to_all | solution.py:160
  588.8 0.9 copy-start.4
  589.9 6.6 %collective-permute-start = (bf16[128,512]{1,0:T(8,128)(2,1)S(1)}, bf16[128,512]{1,0:T(8,128)(2,1)S(1)}, u32[]{:S(2)}, u32[]{:S(2)}) collective-permute-start(bf16[128,512]{1,0:T(8,128)(2,1)S(1)} %get-tuple-element.19), channel_id=1, source_target_pairs={{0,64},{64,0},{1,65},{65,1},{2,66},{66,2},{3,67},{67,3},{4,68},{68... | collective-permute-start | bytes 393224 | tf_op jit(solution)/shard_map/ppermute | solution.py:21
Sparse Core Ops, SparseCore 0:
  37.8 102.9 all-gather.2
  165.8 131.3 reduce-scatter.2
  348.2 66.9 all-gather.4
  439.6 130.8 reduce-scatter.4
